TPU v7x, 32 devices: a whole 2x2x4 slice. The times are simulated.
32 devices in a mesh: seq: 4 (over z), row: 2 (over x), col: 4 (over y, core).
Axes of the slice: x: 2, y: 2, z: 4, core: 2. Of those that a mesh axis runs over, the one named last changes fastest.
Arguments:
- grads: bfloat16 [1024, 28672], P('row', ('seq', 'col')), may hold values from -6 to 6
- acts: bfloat16 [1024, 8192], P(('seq', 'col'), 'row'), may hold values from -6 to 6
- out_basis: bfloat16 [28672, 28672], P(('seq', 'col'), 'row'), may hold values from -0.03125 to 0.03125
- in_basis: bfloat16 [8192, 8192], P('row', ('seq', 'col')), may hold values from -0.0625 to 0.0625
- lengths: int32 [4], replicated, may hold values from 1 to 256, 768 in all
Outputs:
- eigenvalues: float32 [28672, 8192], P('row', ('seq', 'col'))
Inputs may be any that keep to these rules, and one draw needn't show every extreme that they name: lengths sum to 768; some sequence is full.
All inputs are finite; a program needn't handle non-finite values.
Results may differ from a plain program's by a relative error of at most 0.0036.
Values may be sent and summed in bfloat16 or wider, within the bound.
No kernel may reach another device: no remote copies, remote signals or barrier semaphores. Data moves between devices by JAX's collectives and lax.ppermute only.
A program may use at most 192 MiB of HBM per device.

v0:
```python
import jax
import jax.numpy as jnp
from jax import lax
from jax.sharding import PartitionSpec as P

SEQ_LEN = 256


def body(grads, acts, out_basis, in_basis, lengths):
    seq_count = lax.axis_size("seq")
    partial_value = jnp.dot(
        lax.all_gather(grads, "row", axis=0, tiled=True),
        out_basis,
        preferred_element_type=jnp.float32,
    )
    shared = lax.psum_scatter(
        partial_value, ("seq", "col"), scatter_dimension=0, tiled=True
    ).astype(jnp.bfloat16)
    grad_proj = lax.all_gather(shared, ("seq", "col"), axis=0, tiled=True)
    act_full = lax.all_gather(acts, ("seq", "col"), axis=0, tiled=True)
    row_count = act_full.shape[0] // lax.axis_size("row")
    act_share = lax.psum_scatter(
        jnp.dot(act_full, in_basis, preferred_element_type=jnp.float32),
        "row",
        scatter_dimension=0,
        tiled=True,
    )
    token_index = lax.axis_index("row") * row_count + jnp.arange(row_count, dtype=jnp.int32)
    seq_owner = token_index // SEQ_LEN
    position = token_index % SEQ_LEN
    seq_ids = jnp.arange(lengths.shape[0], dtype=jnp.int32)
    seq_length = jnp.sum(
        jnp.where(seq_owner[:, None] == seq_ids[None, :], lengths[None, :], 0), axis=1
    )
    is_live = (position < seq_length).astype(jnp.float32)
    act_rows = (act_share * is_live[:, None]).astype(jnp.bfloat16)
    act_proj = lax.all_gather(act_rows, "row", axis=0, tiled=True)
    grad_three = grad_proj.reshape(seq_count, SEQ_LEN, grad_proj.shape[1])
    act_three = act_proj.reshape(seq_count, SEQ_LEN, act_proj.shape[1])

    def accumulate(total, pair):
        grad_seq = lax.dot_general(
            pair[0], pair[1], (((0,), (0,)), ((), ())), preferred_element_type=jnp.float32
        )
        return (total + grad_seq * grad_seq, None)

    start_total = jnp.zeros((grad_proj.shape[1], act_proj.shape[1]), jnp.float32)
    total, unused = lax.scan(accumulate, start_total, (grad_three, act_three))
    return total / (seq_count * SEQ_LEN)


def solution(mesh):
    in_specs = (
        P("row", ("seq", "col")),
        P(("seq", "col"), "row"),
        P(("seq", "col"), "row"),
        P("row", ("seq", "col")),
        P(),
    )
    out_specs = P("row", ("seq", "col"))
    return jax.shard_map(body, mesh=mesh, in_specs=in_specs, out_specs=out_specs, check_vma=False)
```

profile of v0, /device:TPU:0, one launch (start us, length us, event | category | flops | bytes accessed | tf_op | source)
XLA Modules:
  0.0 1026.4 jit_solution(2737312579928235506)
XLA Ops:
  6.5 0.0 all-gather.9.cloned.1.call-start
  6.5 0.7 all-gather.9.cloned.1.call-update
  7.3 0.0 all-gather.5.cloned.1.call-start
  7.3 0.7 all-gather.5.cloned.1.call-update
  8.0 0.0 reduce-scatter.5.cloned.1.call-start
  8.1 78.5 %all-gather.9.cloned.1.call-done = bf16[1024,4096]{1,0:T(8,128)(2,1)} async-done(((bf16[64,4096]{1,0:T(8,128)(2,1)}), bf16[1024,4096]{1,0:T(8,128)(2,1)}) %all-gather.9.cloned.1.call-update) | async-done | bytes 8388624 | tf_op jit(solution)/shard_map/all_gather | solution.py:20
  86.5 10.4 %fusion.11 = f32[1024,512]{1,0:T(8,128)} fusion(bf16[1024,4096]{1,0:T(8,128)(2,1)} %all-gather.9.cloned.1.call-done, bf16[4096,512]{1,0:T(8,128)(2,1)} %param.10), kind=kOutput, calls=%fused_computation.23 | convolution fusion | flops 4294967296 | bytes 14680064 | tf_op jit(solution)/shard_map/dot_general | solution.py:23
  96.9 0.0 reduce-scatter.5.cloned.1.call-update
  97.0 0.0 reduce-scatter.3.cloned.1.call-start
  97.0 40.5 %all-gather.5.cloned.1.call-done = bf16[1024,1792]{1,0:T(8,128)(2,1)} async-done(((bf16[512,1792]{1,0:T(8,128)(2,1)}), bf16[1024,1792]{1,0:T(8,128)(2,1)}) %all-gather.5.cloned.1.call-update) | async-done | bytes 3670032 | tf_op jit(solution)/shard_map/all_gather | solution.py:12
  137.5 61.7 %fusion.10 = f32[1024,14336]{1,0:T(8,128)} fusion(bf16[1024,1792]{1,0:T(8,128)(2,1)} %all-gather.5.cloned.1.call-done, bf16[1792,14336]{1,0:T(8,128)(2,1)} %param.9), kind=kOutput, calls=%fused_computation.22 | convolution fusion | flops 52613349376 | bytes 113770496 | tf_op jit(solution)/shard_map/dot_general | solution.py:11
  199.2 0.0 copy-start
  199.2 0.0 reduce-scatter.3.cloned.1.call-update
  199.3 0.0 all-gather.11.cloned.1.call-start
  199.3 0.6 copy-done
  199.9 0.1 select_reduce_fusion
  200.0 0.0 reduce-scatter.5.cloned.1.call-done
  200.0 2.2 multiply_convert_fusion
  202.2 0.0 all-gather.11.cloned.1.call-update
  202.2 0.0 all-gather.7.cloned.1.call-start
  202.2 538.7 %reduce-scatter.3.cloned.1.call-done = f32[64,14336]{1,0:T(8,128)} async-done(((f32[1024,14336]{1,0:T(8,128)}), f32[64,14336]{1,0:T(8,128)}) %reduce-scatter.3.cloned.1.call-update) | async-done | bytes 3670032 | tf_op jit(solution)/shard_map/reduce_scatter | solution.py:16
  740.9 3.5 convert_element_type.13
  744.4 0.0 all-gather.7.cloned.1.call-update
  744.5 18.3 %all-gather.11.cloned.1.call-done = bf16[1024,512]{1,0:T(8,128)(2,1)} async-done(((bf16[512,512]{1,0:T(8,128)(2,1)}), bf16[1024,512]{1,0:T(8,128)(2,1)}) %all-gather.11.cloned.1.call-update) | async-done | bytes 1048592 | tf_op jit(solution)/shard_map/all_gather | solution.py:37
  762.7 149.8 %all-gather.7.cloned.1.call-done = bf16[1024,14336]{1,0:T(8,128)(2,1)} async-done(((bf16[64,14336]{1,0:T(8,128)(2,1)}), bf16[1024,14336]{1,0:T(8,128)(2,1)}) %all-gather.7.cloned.1.call-update) | async-done | bytes 29360144 | tf_op jit(solution)/shard_map/all_gather | solution.py:19
  912.5 85.2 %while.11 = (s32[]{:T(128)}, f32[14336,512]{1,0:T(8,128)}, bf16[4,256,14336]{2,1,0:T(8,128)(2,1)}, bf16[4,256,512]{2,1,0:T(8,128)(2,1)}, s32[]{:T(128)}, /*index=5*/s32[]{:T(128)}) while((s32[]{:T(128)}, f32[14336,512]{1,0:T(8,128)}, bf16[4,256,14336]{2,1,0:T(8,128)(2,1)}, bf16[4,256,512]{2,1,0:T(8,128)(2,1)}, s32[]{:T(128)}, ...), condition=%wide.region_4.5_spmd.clone, body=%wide.region_3.4_spmd.clone.sunk | while | flops 3780116480 | bytes 66323532 | solution.py:48
  912.5 13.2 %select_add_fusion.2 = f32[14336,512]{1,0:T(8,128)} fusion(f32[14336,512]{1,0:T(8,128)} %get-tuple-element.83, pred[]{:T(512)S(6)} %compare.14, bf16[4,256,14336]{2,1,0:T(8,128)(2,1)} %get-tuple-element.90, s32[]{:T(128)} %get-tuple-element.82, bf16[4,256,512]{2,1,0:T(8,128)(2,1)} %get-tuple-element.91), kind=kOutput, calls=%fused_computation.clone.1 | convolution fusion | flops 3780116480 | bytes 66323456 | tf_op jit(solution)/shard_map/while/body/eval_jaxpr/dot_general | solution.py:42
  925.7 24.0 %select_add_fusion.2 = f32[14336,512]{1,0:T(8,128)} fusion(f32[14336,512]{1,0:T(8,128)} %get-tuple-element.83, pred[]{:T(512)S(6)} %compare.14, bf16[4,256,14336]{2,1,0:T(8,128)(2,1)} %get-tuple-element.90, s32[]{:T(128)} %get-tuple-element.82, bf16[4,256,512]{2,1,0:T(8,128)(2,1)} %get-tuple-element.91), kind=kOutput, calls=%fused_computation.clone.1 | convolution fusion | flops 3780116480 | bytes 66323456 | tf_op jit(solution)/shard_map/while/body/eval_jaxpr/dot_general | solution.py:42
  949.7 24.0 %select_add_fusion.2 = f32[14336,512]{1,0:T(8,128)} fusion(f32[14336,512]{1,0:T(8,128)} %get-tuple-element.83, pred[]{:T(512)S(6)} %compare.14, bf16[4,256,14336]{2,1,0:T(8,128)(2,1)} %get-tuple-element.90, s32[]{:T(128)} %get-tuple-element.82, bf16[4,256,512]{2,1,0:T(8,128)(2,1)} %get-tuple-element.91), kind=kOutput, calls=%fused_computation.clone.1 | convolution fusion | flops 3780116480 | bytes 66323456 | tf_op jit(solution)/shard_map/while/body/eval_jaxpr/dot_general | solution.py:42
  973.7 24.0 %select_add_fusion.2 = f32[14336,512]{1,0:T(8,128)} fusion(f32[14336,512]{1,0:T(8,128)} %get-tuple-element.83, pred[]{:T(512)S(6)} %compare.14, bf16[4,256,14336]{2,1,0:T(8,128)(2,1)} %get-tuple-element.90, s32[]{:T(128)} %get-tuple-element.82, bf16[4,256,512]{2,1,0:T(8,128)(2,1)} %get-tuple-element.91), kind=kOutput, calls=%fused_computation.clone.1 | convolution fusion | flops 3780116480 | bytes 66323456 | tf_op jit(solution)/shard_map/while/body/eval_jaxpr/dot_general | solution.py:42
  997.7 21.9 %broadcast_multiply_fusion = f32[14336,512]{1,0:T(8,128)} fusion(f32[14336,512]{1,0:T(8,128)} %get-tuple-element.27), kind=kLoop, calls=%fused_computation.6 | loop fusion | flops 7340032 | bytes 58720256 | tf_op jit(solution)/shard_map/div | solution.py:49
  (3 shorter events, 0.0 us)
Async XLA Ops:
  6.5 80.0 %all-gather.9.cloned.1.call-start = ((), (), s32[]{:S(2)}) async-start(), calls=%async_computation.5 | async-start | bytes 8912896 | tf_op jit(solution)/shard_map/all_gather | solution.py:20
  7.3 130.3 %all-gather.5.cloned.1.call-start = ((), (), s32[]{:S(2)}) async-start(), calls=%async_computation.2 | async-start | bytes 5505024 | tf_op jit(solution)/shard_map/all_gather | solution.py:12
  8.0 192.0 %reduce-scatter.5.cloned.1.call-start = ((), (), s32[]{:S(2)}) async-start(), calls=%async_computation.6 | async-start | bytes 3145728 | tf_op jit(solution)/shard_map/reduce_scatter | solution.py:22
  97.0 644.0 %reduce-scatter.3.cloned.1.call-start = ((), (), s32[]{:S(2)}) async-start(), calls=%async_computation.3 | async-start | bytes 62390272 | tf_op jit(solution)/shard_map/reduce_scatter | solution.py:16
  199.2 0.7 copy-start
  199.3 563.5 %all-gather.11.cloned.1.call-start = ((), (), s32[]{:S(2)}) async-start(), calls=%async_computation.7 | async-start | bytes 1572864 | tf_op jit(solution)/shard_map/all_gather | solution.py:37
  202.2 710.3 %all-gather.7.cloned.1.call-start = ((), (), s32[]{:S(2)}) async-start(), calls=%async_computation.4 | async-start | bytes 31195136 | tf_op jit(solution)/shard_map/all_gather | solution.py:19
Sparse Core Ops, SparseCore 0:
  9.5 77.0 all-gather.8
  88.1 49.3 all-gather.4
  139.8 31.8 reduce-scatter.4
  199.4 541.5 reduce-scatter.2
  742.3 20.3 all-gather.10
  764.2 148.2 all-gather.6
where the time goes:
time: 1030 us
  waiting for transfers between devices  827 us (80%)
  matrix products  157 us (15%)
  other arithmetic  27.6 us (3%)
  between operations  13.5 us (1%)
    reduce_scatter x1, waiting for transfers between devices, body(): lax.psum_scatter(partial_value, ('seq', 'col'), scatter_dimension=0, tile...  539 us
    all_gather x1, waiting for transfers between devices, body(): grad_proj = lax.all_gather(shared, ('seq', 'col'), axis=0, tiled=True)  150 us
    dot_general x4, matrix products, accumulate(): lax.dot_general(pair[0], pair[1], (((0,), (0,)), ((), ())), preferred_ele...  85.2 us
    all_gather x1, waiting for transfers between devices, body(): act_full = lax.all_gather(acts, ('seq', 'col'), axis=0, tiled=True)  78.5 us
    dot_general x1, matrix products, body(): jnp.dot(lax.all_gather(grads, 'row', axis=0, tiled=True), out_basis, pref...  61.7 us
    all_gather x1, waiting for transfers between devices, body(): lax.all_gather(grads, 'row', axis=0, tiled=True)  40.5 us
    div x1, other arithmetic, body(): return total / (seq_count * SEQ_LEN)  21.9 us
  transfers between devices with their start and end apart: 6, of which 5 were waited for; matrix products, arithmetic and copies ran while one was open for 8% of the time, Pallas kernels for 0%

commit v1 on v0

--- a/solution.py
+++ b/solution.py
@@ -16,7 +16,13 @@
     shared = lax.psum_scatter(
         partial_value, ("seq", "col"), scatter_dimension=0, tiled=True
     ).astype(jnp.bfloat16)
-    grad_proj = lax.all_gather(shared, ("seq", "col"), axis=0, tiled=True)
+    current_block = lax.all_to_all(
+        jnp.stack([shared for _ in range(lax.axis_size(("seq", "col")))]),
+        axis_name=("seq", "col"),
+        split_axis=0,
+        concat_axis=0,
+    )
+    grad_proj = jnp.concatenate(current_block, 0)
     act_full = lax.all_gather(acts, ("seq", "col"), axis=0, tiled=True)
     row_count = act_full.shape[0] // lax.axis_size("row")
     act_share = lax.psum_scatter(

time: 1030 us -> 1480 us (1.44)
  the two profiles are of different devices: /device:TPU:0 before, /device:TPU:13 now
where the time goes in v1:
time: 1480 us
  waiting for transfers between devices  1260 us (85%)
  matrix products  157 us (11%)
  other arithmetic  26.4 us (2%)
    reduce_scatter x1, waiting for transfers between devices, body(): lax.psum_scatter(partial_value, ('seq', 'col'), scatter_dimension=0, tile...  540 us
    all_gather x1, waiting for transfers between devices, body(): act_full = lax.all_gather(acts, ('seq', 'col'), axis=0, tiled=True)  349 us
    all_to_all x1, waiting for transfers between devices, body(): lax.all_to_all(jnp.stack([shared for _ in range(lax.axis_size(('seq', 'co...  232 us
    dot_general x4, matrix products, accumulate(): lax.dot_general(pair[0], pair[1], (((0,), (0,)), ((), ())), preferred_ele...  85.2 us
    reduce_scatter x1, waiting for transfers between devices, body(): lax.psum_scatter(jnp.dot(act_full, in_basis, preferred_element_type=jnp.f...  66.3 us
    dot_general x1, matrix products, body(): jnp.dot(lax.all_gather(grads, 'row', axis=0, tiled=True), out_basis, pref...  61.8 us
    all_gather x1, waiting for transfers between devices, body(): lax.all_gather(grads, 'row', axis=0, tiled=True)  53.4 us
  transfers between devices with their start and end apart: 6, of which 6 were waited for; matrix products, arithmetic and copies ran while one was open for 1% of the time, Pallas kernels for 0%

profile of v1, /device:TPU:13, one launch (start us, length us, event | category | flops | bytes accessed | tf_op | source)
XLA Modules:
  0.0 1479.0 jit_solution(18233097945720318350)
XLA Ops:
  6.5 0.0 all-gather.4.cloned.1.call-start
  6.5 0.7 all-gather.4.cloned.1.call-update
  7.3 0.0 reduce-scatter.3.cloned.1.call-start
  7.3 53.4 %all-gather.4.cloned.1.call-done = bf16[1024,1792]{1,0:T(8,128)(2,1)} async-done(((bf16[512,1792]{1,0:T(8,128)(2,1)}), bf16[1024,1792]{1,0:T(8,128)(2,1)}) %all-gather.4.cloned.1.call-update) | async-done | bytes 3670032 | tf_op jit(solution)/shard_map/all_gather | solution.py:12
  60.7 61.8 %fusion.10 = f32[1024,14336]{1,0:T(8,128)} fusion(bf16[1024,1792]{1,0:T(8,128)(2,1)} %all-gather.4.cloned.1.call-done, bf16[1792,14336]{1,0:T(8,128)(2,1)} %param.9), kind=kOutput, calls=%fused_computation.22 | convolution fusion | flops 52613349376 | bytes 113770496 | tf_op jit(solution)/shard_map/dot_general | solution.py:11
  122.5 0.0 reduce-scatter.3.cloned.1.call-update
  122.5 540.0 %reduce-scatter.3.cloned.1.call-done = f32[64,14336]{1,0:T(8,128)} async-done(((f32[1024,14336]{1,0:T(8,128)}), f32[64,14336]{1,0:T(8,128)}) %reduce-scatter.3.cloned.1.call-update) | async-done | bytes 3670032 | tf_op jit(solution)/shard_map/reduce_scatter | solution.py:16
  662.5 2.2 convert_element_type.13
  664.7 10.1 stack.2
  674.8 8.2 all-to-all-start
  683.0 0.0 copy-start
  683.0 0.0 all-gather.6.cloned.1.call-start
  683.1 0.7 all-gather.6.cloned.1.call-update
  683.8 0.0 reduce-scatter.5.cloned.1.call-start
  683.8 349.4 %all-gather.6.cloned.1.call-done = bf16[1024,4096]{1,0:T(8,128)(2,1)} async-done(((bf16[64,4096]{1,0:T(8,128)(2,1)}), bf16[1024,4096]{1,0:T(8,128)(2,1)}) %all-gather.6.cloned.1.call-update) | async-done | bytes 8388624 | tf_op jit(solution)/shard_map/all_gather | solution.py:26
  1033.2 10.4 fusion.11
  1043.5 0.0 reduce-scatter.5.cloned.1.call-update
  1043.6 0.0 all-gather.8.cloned.1.call-start
  1043.6 0.0 copy-done
  1043.6 0.1 select_reduce_fusion
  1043.7 66.3 %reduce-scatter.5.cloned.1.call-done = f32[512,512]{1,0:T(8,128)} async-done(((f32[1024,512]{1,0:T(8,128)}), f32[512,512]{1,0:T(8,128)}) %reduce-scatter.5.cloned.1.call-update) | async-done | bytes 1048592 | tf_op jit(solution)/shard_map/reduce_scatter | solution.py:28
  1110.0 2.2 multiply_convert_fusion
  1112.2 0.0 all-gather.8.cloned.1.call-update
  1112.2 21.4 %all-gather.8.cloned.1.call-done = bf16[1024,512]{1,0:T(8,128)(2,1)} async-done(((bf16[512,512]{1,0:T(8,128)(2,1)}), bf16[1024,512]{1,0:T(8,128)(2,1)}) %all-gather.8.cloned.1.call-update) | async-done | bytes 1048592 | tf_op jit(solution)/shard_map/all_gather | solution.py:43
  1133.7 231.7 %all-to-all-done = bf16[16,64,14336]{2,1,0:T(8,128)(2,1)} async-done(((bf16[16,64,14336]{2,1,0:T(8,128)(2,1)}), bf16[16,64,14336]{2,1,0:T(8,128)(2,1)}, u32[]{:S(2)}, u32[]{:S(2)}) %all-to-all-start) | async-done | bytes 29360160 | tf_op jit(solution)/shard_map/all_to_all | solution.py:19
  1365.4 85.2 %while.11 = (s32[]{:T(128)}, f32[14336,512]{1,0:T(8,128)}, bf16[4,256,14336]{2,1,0:T(8,128)(2,1)}, bf16[4,256,512]{2,1,0:T(8,128)(2,1)}, s32[]{:T(128)}, /*index=5*/s32[]{:T(128)}) while((s32[]{:T(128)}, f32[14336,512]{1,0:T(8,128)}, bf16[4,256,14336]{2,1,0:T(8,128)(2,1)}, bf16[4,256,512]{2,1,0:T(8,128)(2,1)}, s32[]{:T(128)}, ...), condition=%wide.region_4.5_spmd.clone, body=%wide.region_3.4_spmd.clone.sunk | while | flops 3780116480 | bytes 66323532 | solution.py:54
  1365.4 13.2 select_add_fusion.2
  1378.6 24.0 %select_add_fusion.2 = f32[14336,512]{1,0:T(8,128)} fusion(f32[14336,512]{1,0:T(8,128)} %get-tuple-element.83, pred[]{:T(512)S(6)} %compare.14, bf16[4,256,14336]{2,1,0:T(8,128)(2,1)} %get-tuple-element.90, s32[]{:T(128)} %get-tuple-element.82, bf16[4,256,512]{2,1,0:T(8,128)(2,1)} %get-tuple-element.91), kind=kOutput, calls=%fused_computation.clone.1 | convolution fusion | flops 3780116480 | bytes 66323456 | tf_op jit(solution)/shard_map/while/body/eval_jaxpr/dot_general | solution.py:48
  1402.6 24.0 %select_add_fusion.2 = f32[14336,512]{1,0:T(8,128)} fusion(f32[14336,512]{1,0:T(8,128)} %get-tuple-element.83, pred[]{:T(512)S(6)} %compare.14, bf16[4,256,14336]{2,1,0:T(8,128)(2,1)} %get-tuple-element.90, s32[]{:T(128)} %get-tuple-element.82, bf16[4,256,512]{2,1,0:T(8,128)(2,1)} %get-tuple-element.91), kind=kOutput, calls=%fused_computation.clone.1 | convolution fusion | flops 3780116480 | bytes 66323456 | tf_op jit(solution)/shard_map/while/body/eval_jaxpr/dot_general | solution.py:48
  1426.6 24.0 %select_add_fusion.2 = f32[14336,512]{1,0:T(8,128)} fusion(f32[14336,512]{1,0:T(8,128)} %get-tuple-element.83, pred[]{:T(512)S(6)} %compare.14, bf16[4,256,14336]{2,1,0:T(8,128)(2,1)} %get-tuple-element.90, s32[]{:T(128)} %get-tuple-element.82, bf16[4,256,512]{2,1,0:T(8,128)(2,1)} %get-tuple-element.91), kind=kOutput, calls=%fused_computation.clone.1 | convolution fusion | flops 3780116480 | bytes 66323456 | tf_op jit(solution)/shard_map/while/body/eval_jaxpr/dot_general | solution.py:48
  1450.6 21.9 %broadcast_multiply_fusion = f32[14336,512]{1,0:T(8,128)} fusion(f32[14336,512]{1,0:T(8,128)} %get-tuple-element.27), kind=kLoop, calls=%fused_computation.6 | loop fusion | flops 7340032 | bytes 58720256 | tf_op jit(solution)/shard_map/div | solution.py:55
  (3 shorter events, 0.0 us)
Async XLA Ops:
  6.5 54.1 %all-gather.4.cloned.1.call-start = ((), (), s32[]{:S(2)}) async-start(), calls=%async_computation.3 | async-start | bytes 5505024 | tf_op jit(solution)/shard_map/all_gather | solution.py:12
  7.3 655.2 %reduce-scatter.3.cloned.1.call-start = ((), (), s32[]{:S(2)}) async-start(), calls=%async_computation.4 | async-start | bytes 62390272 | tf_op jit(solution)/shard_map/reduce_scatter | solution.py:16
  674.8 690.5 %all-to-all-start = ((bf16[16,64,14336]{2,1,0:T(8,128)(2,1)}), bf16[16,64,14336]{2,1,0:T(8,128)(2,1)}, u32[]{:S(2)}, u32[]{:S(2)}) async-start(bf16[16,64,14336]{2,1,0:T(8,128)(2,1)} %stack.2), calls=%async_computation.1 | async-start | bytes 58720256 | tf_op jit(solution)/shard_map/all_to_all | solution.py:19
  683.0 360.6 %copy-start = (s32[4]{0:T(128)S(1)}, s32[4]{0:T(128)}, u32[]{:S(2)}) copy-start(s32[4]{0:T(128)} %param.11) | copy-start | bytes 52
  683.0 350.2 %all-gather.6.cloned.1.call-start = ((), (), s32[]{:S(2)}) async-start(), calls=%async_computation.5 | async-start | bytes 8912896 | tf_op jit(solution)/shard_map/all_gather | solution.py:26
  683.8 426.3 %reduce-scatter.5.cloned.1.call-start = ((), (), s32[]{:S(2)}) async-start(), calls=%async_computation.6 | async-start | bytes 3145728 | tf_op jit(solution)/shard_map/reduce_scatter | solution.py:28
  1043.6 90.1 %all-gather.8.cloned.1.call-start = ((), (), s32[]{:S(2)}) async-start(), calls=%async_computation.7 | async-start | bytes 1572864 | tf_op jit(solution)/shard_map/all_gather | solution.py:43
Sparse Core Ops, SparseCore 0:
  8.9 51.7 all-gather.3
  122.6 539.8 reduce-scatter.2
  686.0 347.1 all-gather.5
  1043.7 66.3 reduce-scatter.4
  1112.4 21.2 all-gather.7
